TPU v7x, 256 devices: a whole 4x4x8 slice. The times are simulated.
256 devices in a mesh: group: 32 (over y, z), pencil: 8 (over x, core).
Axes of the slice: x: 4, y: 4, z: 8, core: 2. Of those that a mesh axis runs over, the one named last changes fastest.
Arguments:
- mult_iterate: float32 [32, 8, 8192], P('group', 'pencil'), may hold values from -6 to 6
- residual: float32 [32, 8, 8192], P('group', 'pencil'), may hold values from -6 to 6
- direction: float32 [32, 8, 8192], P('group', 'pencil'), may hold values from -6 to 6
- mult_scale: float32 [32, 8, 8192], P('group', 'pencil'), may hold values from 0.5 to 18
- eigen_basis: float32 [128, 3, 64, 64], P('group'), may hold values from -1 to 1
- eigen_values: float32 [128, 3, 64], P('group'), may hold values from 0.2 to 2
- elastic_coef: float32 [128, 3, 3], P('group'), may hold values from 0.5 to 2
- coarse_inverse: float32 [1024, 1024], replicated, may hold values from -1 to 2.5
- send_pos: int32 [32, 8, 16384], P('group', 'pencil'), may hold values from 0 to 24191, as said below
- pair_slots: int32 [32, 8, 2, 8192], P('group', 'pencil'), may hold values from 0 to 16383, as said below
- prim_rows: int32 [32, 8, 32], P('group', 'pencil'), may hold values from 0 to 16383, as said below
- coarse_idx: int32 [32, 8, 32], P('group', 'pencil'), may hold values from 0 to 1023
Outputs:
- new_iterate: float32 [32, 8, 8192], P('group', 'pencil')
- new_residual: float32 [32, 8, 8192], P('group', 'pencil')
- new_direction: float32 [32, 8, 8192], P('group', 'pencil')
Inputs may be any that keep to these rules, and one draw needn't show every extreme that they name: `send_pos`: distinct within each block (g, s). `pair_slots`: in each block (g, s) the two rows together hold every number of 0 to 16383 once. `prim_rows`: distinct within each block (g, s).
All inputs are finite; a program needn't handle non-finite values.
Results may differ from a plain program's by a relative error of at most 0.0003.
Values sent between devices are 32-bit elements; how exact they have to be, the bound alone decides.
No kernel may reach another device: no remote copies, remote signals or barrier semaphores. Data moves between devices by JAX's collectives and lax.ppermute only.
A program may use at most 128 MiB of HBM per device.

v0:
```python
import jax
import jax.numpy as jnp
from jax import lax
from jax.sharding import PartitionSpec as P


def cycle_slot(index, extent):
    cycle_size = 4 * extent - 4
    plane_index = index // cycle_size
    cycle_spot = index % cycle_size
    side_slot = jnp.where(
        cycle_spot < extent,
        cycle_spot,
        jnp.where(
            cycle_spot < 2 * extent - 2,
            cycle_spot + 1,
            jnp.where(cycle_spot < 3 * extent - 4, cycle_spot + 3, cycle_spot + 4),
        ),
    )
    return plane_index * 4 * extent + side_slot


def cycle_to_volume(cycles, extent):
    sides = cycles.reshape(cycles.shape[:-1] + (4, extent))
    count = jnp.arange(extent, dtype=jnp.int32)
    first_edge = (count == 0).astype(jnp.float32)
    last_edge = (count == extent - 1).astype(jnp.float32)
    plane = sides[..., 0, None, :] * first_edge[:, None]
    plane = plane + sides[..., 1, :, None] * first_edge[None, :]
    plane = plane + sides[..., 2, :, None] * last_edge[None, :]
    return plane + sides[..., 3, None, :] * last_edge[:, None]


def volume_to_cycle(volume):
    sides = jnp.stack(
        [volume[..., 0, :], volume[..., :, 0], volume[..., :, -1], volume[..., -1, :]], axis=-2
    )
    return sides.reshape(volume.shape[:-2] + (4 * volume.shape[-1],))


def spectrum(coeffs, along_x, along_y, along_z):
    first = coeffs[None, :, :, 0, None, None] * along_x.T[:, :, None, None, None]
    second = coeffs[None, :, :, 1, None, None] * along_y[None, :, None, :, None]
    third = coeffs[None, :, :, 2, None, None] * along_z[None, :, None, None, :]
    return first + second + third


def forward_yz(volume, basis):
    highest = lax.Precision.HIGHEST
    step_one = jnp.einsum("xpcyz,pzk->xpcyk", volume, basis[:, 2], precision=highest)
    return jnp.einsum("xpcyk,pyj->xpcjk", step_one, basis[:, 1], precision=highest)


def backward_yz(volume, basis):
    highest = lax.Precision.HIGHEST
    step_one = jnp.einsum("xpcjk,pyj->xpcyk", volume, basis[:, 1], precision=highest)
    return jnp.einsum("xpcyk,pzk->xpcyz", step_one, basis[:, 2], precision=highest)


def load_slab(arrived_rows, positions, slab_shape):
    cycle_total = slab_shape[0] * slab_shape[1] * slab_shape[2] * 4 * slab_shape[3]
    cycles = jnp.zeros((cycle_total,), jnp.float32).at[positions].set(arrived_rows)
    cycles = cycles.reshape(slab_shape[0], slab_shape[1], slab_shape[2], 4 * slab_shape[3])
    return cycle_to_volume(cycles, slab_shape[3])


def apply_inverse(arrived_rows, cycle_cells, basis, values, coeffs):
    highest = lax.Precision.HIGHEST
    pencils = lax.axis_size("pencil")
    extent = basis.shape[-1]
    patches = basis.shape[0]
    components = coeffs.shape[1]
    slab_x = extent // pencils
    slab_shape = (slab_x, patches, components, extent, extent)
    my_slab = lax.axis_index("pencil")
    row_start = my_slab * slab_x
    positions = cycle_slot(cycle_cells, extent)
    partial_yz = forward_yz(load_slab(arrived_rows, positions, slab_shape), basis)
    columns = lax.all_to_all(
        partial_yz.reshape(slab_x, patches, components, extent * extent),
        "pencil",
        split_axis=3,
        concat_axis=0,
        tiled=True,
    )
    columns = columns.reshape(extent, patches, components, slab_x, extent)
    spectral = jnp.einsum("xpcjk,pxi->ipcjk", columns, basis[:, 0], precision=highest)
    along_y = lax.dynamic_slice_in_dim(values[:, 1], row_start, slab_x, 1)
    scaled = spectral / spectrum(coeffs, values[:, 0], along_y, values[:, 2])
    mixed = jnp.einsum("ipcjk,pxi->xpcjk", scaled, basis[:, 0], precision=highest)
    mixed = mixed.reshape(extent, patches, components, slab_x * extent)
    back_x = lax.all_to_all(mixed, "pencil", split_axis=0, concat_axis=3, tiled=True).reshape(
        slab_shape
    )
    displace = backward_yz(back_x, basis)
    return volume_to_cycle(displace).reshape(-1)[positions]


def body(
    mult_iterate,
    residual,
    direction,
    mult_scale,
    eigen_basis,
    eigen_values,
    elastic_coef,
    coarse_inverse,
    send_pos,
    pair_slots,
    prim_rows,
    coarse_idx,
):
    highest = lax.Precision.HIGHEST
    groups = lax.axis_size("group")
    iterate_now = mult_iterate[0, 0]
    resid_now = residual[0, 0]
    search_dir = direction[0, 0]
    scale_now = mult_scale[0, 0]
    pair_rows = pair_slots[0, 0]
    cycle_cells = send_pos[0, 0]
    primal = prim_rows[0, 0]
    coarse_ids = coarse_idx[0, 0]
    rows_count = cycle_cells.shape[0]
    per_owner = rows_count // groups
    coarse_count = coarse_inverse.shape[0]
    old_part = jnp.sum(resid_now * scale_now * resid_now)
    old_norm = lax.psum(old_part, ("group", "pencil"))
    back_rows = (
        jnp.zeros((rows_count,), jnp.float32)
        .at[pair_rows[0]]
        .set(search_dir)
        .at[pair_rows[1]]
        .set(-search_dir)
    )
    arrived_rows = lax.all_to_all(
        back_rows.reshape(groups, per_owner), "group", split_axis=0, concat_axis=0, tiled=True
    ).reshape(rows_count)
    picked = apply_inverse(arrived_rows, cycle_cells, eigen_basis, eigen_values, elastic_coef)
    onehot = (coarse_ids[:, None] == jnp.arange(coarse_count, dtype=jnp.int32)[None, :]).astype(
        jnp.float32
    )
    local_coarse = jnp.dot(picked[primal], onehot, precision=highest)
    total_coarse = lax.psum(local_coarse, ("group", "pencil"))
    lifted = jnp.dot(coarse_inverse, total_coarse, precision=highest)
    sent_rows = picked.at[primal].add(jnp.dot(onehot, lifted, precision=highest))
    owner_rows = lax.all_to_all(
        sent_rows.reshape(groups, per_owner), "group", split_axis=0, concat_axis=0, tiled=True
    ).reshape(rows_count)
    mapped = owner_rows[pair_rows[0]] - owner_rows[pair_rows[1]]
    curvature = lax.psum(jnp.sum(search_dir * mapped), ("group", "pencil"))
    step_size = old_norm / curvature
    iterate_next = iterate_now + step_size * search_dir
    resid_next = resid_now - step_size * mapped
    precond = scale_now * resid_next
    norm_next = lax.psum(jnp.sum(resid_next * precond), ("group", "pencil"))
    search_next = precond + norm_next / old_norm * search_dir
    return (iterate_next[None, None], resid_next[None, None], search_next[None, None])


def solution(mesh):
    in_specs = (
        P("group", "pencil", None),
        P("group", "pencil", None),
        P("group", "pencil", None),
        P("group", "pencil", None),
        P("group", None, None, None),
        P("group", None, None),
        P("group", None, None),
        P(),
        P("group", "pencil", None),
        P("group", "pencil", None, None),
        P("group", "pencil", None),
        P("group", "pencil", None),
    )
    out_specs = (P("group", "pencil", None), P("group", "pencil", None), P("group", "pencil", None))
    return jax.shard_map(body, mesh=mesh, in_specs=in_specs, out_specs=out_specs, check_vma=False)
```

profile of v0, /device:TPU:1, one launch (start us, length us, event | category | flops | bytes accessed | tf_op | source)
XLA Modules:
  0.0 876.2 jit_solution(14388846261782737221)
XLA Ops:
  0.6 1.0 compare_select_fusion.4
  1.7 0.8 neg.3
  2.4 31.2 %scatter_custom_fusion = f32[16384]{0:T(1024)} fusion(s32[8192]{0:T(1024)S(1)} %bitcast.164, f32[8192]{0:T(1024)} %bitcast.154, f32[]{:T(128)} %constant.16.clone.1), kind=kCustom, calls=%fused_computation.81 | custom fusion | bytes 66048 | tf_op jit(solution)/shard_map/scatter | solution.py:131
  33.7 31.9 %scatter_fusion = f32[16384]{0:T(1024)} fusion(f32[16384]{0:T(1024)} %scatter_custom_fusion, s32[8192]{0:T(1024)S(1)} %bitcast.151, f32[8192]{0:T(1024)S(1)} %neg.3), kind=kCustom, calls=%fused_computation.5 | custom fusion | bytes 131072 | tf_op jit(solution)/shard_map/scatter | solution.py:133
  65.6 12.0 %all-to-all-start = ((f32[32,1,512]{2,1,0:T(1,128)}), f32[32,1,512]{2,1,0:T(1,128)S(1)}, u32[]{:S(2)}, u32[]{:S(2)}) async-start(f32[32,1,512]{2,1,0:T(1,128)} %bitcast.11), calls=%async_computation | async-start | bytes 131072 | tf_op jit(solution)/shard_map/all_to_all | solution.py:135
  77.6 0.8 compare_select_fusion
  78.5 8.0 all-to-all-done
  86.5 60.8 %scatter_custom_fusion.2 = f32[24576]{0:T(1024)S(1)} fusion(s32[16384]{0:T(1024)S(1)} %bitcast.160, f32[16384]{0:T(1024)S(1)} %bitcast.167, f32[]{:T(128)} %constant.16.clone.1), kind=kCustom, calls=%fused_computation.72 | custom fusion | bytes 98308 | tf_op jit(solution)/shard_map/scatter | solution.py:62
  147.3 0.1 reshape_reshape.6
  147.4 0.1 fusion.59
  147.7 4.0 fusion.8
  151.7 5.2 fusion.16
  156.9 34.6 %copy.135 = f32[8,4,3,64,64]{0,1,2,4,3:T(4,128)} copy(f32[8,4,3,64,64]{3,4,2,0,1:T(8,128)S(1)} %fusion.16) | data formatting | bytes 3145728 | tf_op jit(solution)/shard_map/reshape | solution.py:80
  191.5 31.9 %reshape.387 = f32[8,1,49152]{2,1,0:T(1,128)} reshape(f32[4096,3,4,8]{3,2,1,0:T(4,128)} %bitcast.146) | data formatting | bytes 3145728
  223.4 6.5 all-to-all-start.1
  229.9 0.1 fusion.60
  230.0 0.1 copy.117
  230.1 0.1 copy.116
  230.2 0.1 copy.118
  230.3 0.1 dynamic-slice_bitcast_fusion
  230.4 0.1 broadcast_multiply_fusion.2
  230.5 0.1 broadcast_multiply_fusion.3
  230.6 0.1 broadcast_multiply_fusion.1
  230.6 0.7 broadcast_add_fusion
  231.3 19.2 %all-to-all-done.1 = f32[8,1,49152]{2,1,0:T(1,128)S(1)} async-done(((f32[8,1,49152]{2,1,0:T(1,128)}), f32[8,1,49152]{2,1,0:T(1,128)S(1)}, u32[]{:S(2)}, u32[]{:S(2)}) %all-to-all-start.1) | async-done | bytes 1572896 | tf_op jit(solution)/shard_map/all_to_all | solution.py:79
  250.5 0.5 broadcast.300
  251.0 4.4 reduce
  255.4 38.7 %reshape.388 = f32[4096,3,4,8]{3,2,1,0:T(4,128)} reshape(f32[8,49152]{1,0:T(8,128)S(1)} %reduce) | data formatting | bytes 3145728
  294.1 20.7 %copy.137 = f32[8,4,3,8,512]{4,0,3,2,1:T(8,128)} copy(f32[8,4,3,8,512]{0,1,2,4,3:T(4,128)} %bitcast.147) | data formatting | bytes 3145728 | tf_op jit(solution)/shard_map/all_to_all | solution.py:79
  314.8 2.6 reshape.305
  317.4 5.1 fusion.5
  322.5 3.2 fusion.2
  325.8 2.1 copy.119
  327.8 4.6 all-to-all-start.2
  332.5 0.6 broadcast_clamp_fusion.1
  333.1 0.6 broadcast_clamp_fusion
  333.7 19.3 %all-to-all-done.2 = f32[64,4,3,512]{3,1,2,0:T(4,128)S(1)} async-done(((f32[64,4,3,512]{3,1,2,0:T(4,128)}), f32[64,4,3,512]{3,1,2,0:T(4,128)S(1)}, u32[]{:S(2)}, u32[]{:S(2)}) %all-to-all-start.2) | async-done | bytes 1572896 | tf_op jit(solution)/shard_map/all_to_all | solution.py:92
  353.0 0.5 copy.152
  353.5 2.1 copy.140
  355.6 2.6 reshape.382
  358.3 5.1 fusion.35
  363.4 5.1 fusion.19
  368.5 2.7 fusion.58
  371.3 2.5 copy.124
  373.9 1.5 copy.125
  375.5 0.2 pad_maximum_fusion
  375.8 0.1 reshape_reshape.7
  375.9 160.4 %gather_fusion = f32[16384]{0:T(1024)} fusion(f32[24576]{0:T(1024)S(1)} %reshape_reshape.7, s32[16384]{0:T(1024)S(1)} %copy-done.8), kind=kCustom, calls=%fused_computation | custom fusion | bytes 196608 | tf_op jit(solution)/shard_map/gather | solution.py:96
  536.3 1.6 gather_fusion.1
  537.9 0.2 fusion.40
  538.1 72.8 %psum.29 = f32[1024]{0:T(1024)S(1)} all-reduce(f32[1024]{0:T(1024)S(1)} %bitcast.172), channel_id=1, replica_groups=mesh['group'=32,'pencil'=8] {'group','pencil'}, use_global_device_ids=true, to_apply=%region_5.6 | all-reduce | flops 1024 | bytes 8192 | tf_op jit(solution)/shard_map/psum | solution.py:143
  610.9 5.6 convolution_bitcast_fusion
  616.6 0.2 convolution_bitcast_fusion.1
  616.8 2.2 scatter_fusion.1
  619.0 5.0 all-to-all-start.3
  624.1 0.6 fusion.51
  624.7 8.2 all-to-all-done.3
  632.9 45.5 %gather_fusion.3 = f32[8192]{0:T(1024)S(1)} fusion(f32[16384]{0:T(1024)S(1)} %bitcast.144, s32[8192]{0:T(1024)S(1)} %copy-done.11), kind=kCustom, calls=%fused_computation.3 | custom fusion | bytes 98304 | tf_op jit(solution)/shard_map/gather | solution.py:149
  678.5 45.5 %gather_fusion.2 = f32[8192]{0:T(1024)S(1)} fusion(f32[16384]{0:T(1024)S(1)} %bitcast.145, s32[8192]{0:T(1024)S(1)} %broadcast_clamp_fusion.2), kind=kCustom, calls=%fused_computation.2 | custom fusion | bytes 98304 | tf_op jit(solution)/shard_map/gather | solution.py:149
  724.0 0.6 multiply_reduce_fusion
  724.6 73.3 %all-reduce = (f32[]{:T(128)}, f32[]{:T(128)}) all-reduce(f32[]{:T(128)} %fusion.51, f32[]{:T(128)} %get-tuple-element.9), channel_id=1, replica_groups=mesh['group'=32,'pencil'=8] {'group','pencil'}, use_global_device_ids=true, to_apply=%region_1.0 | all-reduce | flops 2 | bytes 16 | tf_op jit(solution)/shard_map/psum | solution.py:127
  799.3 0.6 fusion.52
  799.9 74.0 %psum.31 = f32[]{:T(128)} all-reduce(f32[]{:T(128)} %get-tuple-element.7), channel_id=1, replica_groups=mesh['group'=32,'pencil'=8] {'group','pencil'}, use_global_device_ids=true, to_apply=%region_10.11 | all-reduce | flops 1 | bytes 8 | tf_op jit(solution)/shard_map/psum | solution.py:155
  875.3 0.7 multiply_add_fusion
  (53 shorter events, 0.4 us)
Async XLA Ops:
  1.6 64.0 %copy-start.1 = (s32[8192,1]{0,1:T(1,128)}, s32[8192,1]{0,1:T(1,128)S(1)}, u32[]{:S(2)}) copy-start(s32[8192,1]{0,1:T(1,128)S(1)} %get-tuple-element.19) | copy-start | bytes 98308
  1.6 63.9 %copy-start.9 = (s32[8192,1]{0,1:T(1,128)}, s32[8192,1]{0,1:T(1,128)S(1)}, u32[]{:S(2)}) copy-start(s32[8192,1]{0,1:T(1,128)S(1)} %get-tuple-element.20) | copy-start | bytes 98308
  33.7 44.0 %copy-start.12 = (s32[1,1,16384]{2,1,0:T(1,128)S(1)}, s32[1,1,16384]{2,1,0:T(1,128)}, u32[]{:S(2)}) copy-start(s32[1,1,16384]{2,1,0:T(1,128)} %param.20) | copy-start | bytes 196612
  33.7 114.0 %copy-start = (f32[4,3,64,64]{3,2,1,0:T(8,128)S(1)}, f32[4,3,64,64]{3,2,1,0:T(8,128)}, u32[]{:S(2)}) copy-start(f32[4,3,64,64]{3,2,1,0:T(8,128)} %param.16) | copy-start | bytes 589828
  65.6 20.9 %all-to-all-start = ((f32[32,1,512]{2,1,0:T(1,128)}), f32[32,1,512]{2,1,0:T(1,128)S(1)}, u32[]{:S(2)}, u32[]{:S(2)}) async-start(f32[32,1,512]{2,1,0:T(1,128)} %bitcast.11), calls=%async_computation | async-start | bytes 131072 | tf_op jit(solution)/shard_map/all_to_all | solution.py:135
  78.4 8.1 copy-start.6
  223.4 6.5 copy-start.13
  223.4 7.0 copy-start.16
  223.4 27.1 %all-to-all-start.1 = ((f32[8,1,49152]{2,1,0:T(1,128)}), f32[8,1,49152]{2,1,0:T(1,128)S(1)}, u32[]{:S(2)}, u32[]{:S(2)}) async-start(f32[8,1,49152]{2,1,0:T(1,128)} %reshape.387), calls=%async_computation.1 | async-start | bytes 3145728 | tf_op jit(solution)/shard_map/all_to_all | solution.py:79
  317.4 5.1 copy-start.14
  325.8 6.7 copy-start.17
  327.8 4.6 copy-start.2
  327.8 5.2 copy-start.7
  327.8 25.2 %all-to-all-start.2 = ((f32[64,4,3,512]{3,1,2,0:T(4,128)}), f32[64,4,3,512]{3,1,2,0:T(4,128)S(1)}, u32[]{:S(2)}, u32[]{:S(2)}) async-start(f32[64,4,3,512]{3,1,2,0:T(4,128)} %copy.119), calls=%async_computation.2 | async-start | bytes 3145728 | tf_op jit(solution)/shard_map/all_to_all | solution.py:92
  371.3 4.6 copy-start.8
  375.9 162.0 %copy-start.18 = (s32[1,1,32]{2,1,0:T(1,128)S(1)}, s32[1,1,32]{2,1,0:T(1,128)}, u32[]{:S(2)}) copy-start(s32[1,1,32]{2,1,0:T(1,128)} %param.23) | copy-start | bytes 388
  536.3 87.7 %copy-start.10 = (s32[8192,1]{0,1:T(1,128)S(1)}, s32[8192,1]{0,1:T(1,128)}, u32[]{:S(2)}) copy-start(s32[8192,1]{0,1:T(1,128)} %copy-done.9) | copy-start | bytes 98308
  536.3 87.7 %copy-start.4 = (f32[1,1,8192]{2,1,0:T(1,128)S(1)}, f32[1,1,8192]{2,1,0:T(1,128)}, u32[]{:S(2)}) copy-start(f32[1,1,8192]{2,1,0:T(1,128)} %param.15) | copy-start | bytes 98308
  536.3 87.7 %copy-start.5 = (f32[1,1,8192]{2,1,0:T(1,128)S(1)}, f32[1,1,8192]{2,1,0:T(1,128)}, u32[]{:S(2)}) copy-start(f32[1,1,8192]{2,1,0:T(1,128)} %param.13) | copy-start | bytes 98308
  536.3 96.6 %copy-start.11 = (s32[8192]{0:T(1024)S(1)}, s32[8192]{0:T(1024)}, u32[]{:S(2)}) copy-start(s32[8192]{0:T(1024)} %broadcast_clamp_fusion.1) | copy-start | bytes 98308
  619.0 13.9 %all-to-all-start.3 = ((f32[32,1,512]{2,1,0:T(1,128)}), f32[32,1,512]{2,1,0:T(1,128)S(1)}, u32[]{:S(2)}, u32[]{:S(2)}) async-start(f32[32,1,512]{2,1,0:T(1,128)} %bitcast.57), calls=%async_computation.3 | async-start | bytes 131072 | tf_op jit(solution)/shard_map/all_to_all | solution.py:146
  678.4 45.6 %copy-start.3 = (f32[1,1,8192]{2,1,0:T(1,128)S(1)}, f32[1,1,8192]{2,1,0:T(1,128)}, u32[]{:S(2)}) copy-start(f32[1,1,8192]{2,1,0:T(1,128)} %param.14) | copy-start | bytes 98308
  678.4 196.8 %copy-start.15 = (f32[1,1,8192]{2,1,0:T(1,128)S(1)}, f32[1,1,8192]{2,1,0:T(1,128)}, u32[]{:S(2)}) copy-start(f32[1,1,8192]{2,1,0:T(1,128)} %param.12) | copy-start | bytes 98308
where the time goes:
time: 881 us; the launch traced here: 876 us
  local copies, waits for them, and re-layouts  521 us (59%)
  blocking collectives  220 us (25%)
  waiting for transfers between devices  54.7 us (6%)
  matrix products  33.9 us (4%)
  starting transfers between devices  28.2 us (3%)
  other arithmetic  14.1 us (2%)
    gather x1, local copies, waits for them, and re-layouts, apply_inverse(): return volume_to_cycle(displace).reshape(-1)[positions]  160 us
    gather x2, local copies, waits for them, and re-layouts, body(): mapped = owner_rows[pair_rows[0]] - owner_rows[pair_rows[1]]  91.1 us
    psum x1, blocking collectives, body(): norm_next = lax.psum(jnp.sum(resid_next * precond), ('group', 'pencil'))  74 us
    psum x1, blocking collectives, body(): old_norm = lax.psum(old_part, ('group', 'pencil'))  73.3 us
    psum x1, blocking collectives, body(): total_coarse = lax.psum(local_coarse, ('group', 'pencil'))  72.8 us
    unnamed x40, local copies, waits for them, and re-layouts  70.6 us
    scatter x2, local copies, waits for them, and re-layouts, body(): back_rows = jnp.zeros((rows_count,), jnp.float32).at[pair_rows[0]].set(se...  63.2 us
    scatter x1, local copies, waits for them, and re-layouts, load_slab(): jnp.zeros((cycle_total,), jnp.float32).at[positions].set(arrived_rows)  60.8 us
  transfers between devices with their start and end apart: 4, of which 4 were waited for; matrix products, arithmetic and copies ran while one was open for 0% of the time, Pallas kernels for 0%

commit v1 on v0

--- a/solution.py
+++ b/solution.py
@@ -140,7 +140,7 @@
         jnp.float32
     )
     local_coarse = jnp.dot(picked[primal], onehot, precision=highest)
-    total_coarse = lax.psum(local_coarse, ("group", "pencil"))
+    total_coarse = jnp.sum(lax.all_gather(local_coarse, ("group", "pencil")), axis=0)
     lifted = jnp.dot(coarse_inverse, total_coarse, precision=highest)
     sent_rows = picked.at[primal].add(jnp.dot(onehot, lifted, precision=highest))
     owner_rows = lax.all_to_all(

time: 881 us -> 924 us (1.049)
  waiting for transfers between devices: 54.7 us -> 152 us
  blocking collectives: 220 us -> 148 us
  between operations: 4 us -> 17.4 us
    all_gather x0 -> x1, waiting for transfers between devices: none -> 96.7 us  [body(): lax.all_gather(local_coarse, ('group', 'pencil'))]
    psum x1 -> x0, blocking collectives: 72.8 us -> none  [body(): total_coarse = lax.psum(local_coarse, ('group', 'pencil'))]
    unnamed x40 -> x38, local copies, waits for them, and re-layouts: 70.6 us -> 70.6 us
  transfers between devices with their start and end apart: 4 -> 5, of which waited for: 4 -> 5; matrix products, arithmetic and copies ran while one was open for 0% -> 0% of each run, Pallas kernels for 0% -> 0%
where the time goes in v1:
time: 924 us; the launch traced here: 919 us
  local copies, waits for them, and re-layouts  522 us (56%)
  waiting for transfers between devices  152 us (16%)
  blocking collectives  148 us (16%)
  matrix products  34.5 us (4%)
  starting transfers between devices  30.6 us (3%)
  between operations  17.4 us (2%)
  other arithmetic  13.6 us (1%)
    gather x1, local copies, waits for them, and re-layouts, apply_inverse(): return volume_to_cycle(displace).reshape(-1)[positions]  160 us
    all_gather x1, waiting for transfers between devices, body(): lax.all_gather(local_coarse, ('group', 'pencil'))  96.7 us
    gather x2, local copies, waits for them, and re-layouts, body(): mapped = owner_rows[pair_rows[0]] - owner_rows[pair_rows[1]]  91.1 us
    psum x1, blocking collectives, body(): old_norm = lax.psum(old_part, ('group', 'pencil'))  74.7 us
    psum x1, blocking collectives, body(): norm_next = lax.psum(jnp.sum(resid_next * precond), ('group', 'pencil'))  73.4 us
    unnamed x38, local copies, waits for them, and re-layouts  70.6 us
    scatter x2, local copies, waits for them, and re-layouts, body(): back_rows = jnp.zeros((rows_count,), jnp.float32).at[pair_rows[0]].set(se...  63.2 us
    scatter x1, local copies, waits for them, and re-layouts, load_slab(): jnp.zeros((cycle_total,), jnp.float32).at[positions].set(arrived_rows)  60.8 us
  transfers between devices with their start and end apart: 5, of which 5 were waited for; matrix products, arithmetic and copies ran while one was open for 0% of the time, Pallas kernels for 0%

profile of v1, /device:TPU:1, one launch (start us, length us, event | category | flops | bytes accessed | tf_op | source)
XLA Modules:
  0.0 918.7 jit_solution(9599632266071139603)
XLA Ops:
  7.2 1.0 compare_select_fusion.4
  8.2 0.8 neg.3
  9.0 31.2 %scatter_custom_fusion = f32[16384]{0:T(1024)} fusion(s32[8192]{0:T(1024)S(1)} %bitcast.164, f32[8192]{0:T(1024)} %bitcast.154, f32[]{:T(128)} %constant.16.clone.1), kind=kCustom, calls=%fused_computation.81 | custom fusion | bytes 66048 | tf_op jit(solution)/shard_map/scatter | solution.py:131
  40.2 31.9 %scatter_fusion = f32[16384]{0:T(1024)} fusion(f32[16384]{0:T(1024)} %scatter_custom_fusion, s32[8192]{0:T(1024)S(1)} %bitcast.151, f32[8192]{0:T(1024)S(1)} %neg.3), kind=kCustom, calls=%fused_computation.5 | custom fusion | bytes 131072 | tf_op jit(solution)/shard_map/scatter | solution.py:133
  72.1 12.0 %all-to-all-start = ((f32[32,1,512]{2,1,0:T(1,128)}), f32[32,1,512]{2,1,0:T(1,128)S(1)}, u32[]{:S(2)}, u32[]{:S(2)}) async-start(f32[32,1,512]{2,1,0:T(1,128)} %bitcast.11), calls=%async_computation | async-start | bytes 131072 | tf_op jit(solution)/shard_map/all_to_all | solution.py:135
  84.2 0.8 compare_select_fusion
  85.0 8.0 all-to-all-done
  93.0 60.8 %scatter_custom_fusion.2 = f32[24576]{0:T(1024)S(1)} fusion(s32[16384]{0:T(1024)S(1)} %bitcast.160, f32[16384]{0:T(1024)S(1)} %bitcast.167, f32[]{:T(128)} %constant.16.clone.1), kind=kCustom, calls=%fused_computation.72 | custom fusion | bytes 98308 | tf_op jit(solution)/shard_map/scatter | solution.py:62
  153.8 0.1 reshape_reshape.6
  153.9 0.1 fusion.59
  154.2 4.0 fusion.8
  158.3 5.2 fusion.16
  163.5 34.5 %copy.165 = f32[8,4,3,64,64]{0,1,2,4,3:T(4,128)} copy(f32[8,4,3,64,64]{3,4,2,0,1:T(8,128)S(1)} %fusion.16) | data formatting | bytes 3145728 | tf_op jit(solution)/shard_map/reshape | solution.py:80
  198.0 31.9 %reshape.388 = f32[8,1,49152]{2,1,0:T(1,128)} reshape(f32[4096,3,4,8]{3,2,1,0:T(4,128)} %bitcast.146) | data formatting | bytes 3145728
  229.8 6.5 all-to-all-start.1
  236.4 0.1 fusion.60
  236.5 0.1 copy.147
  236.6 0.1 copy.146
  236.7 0.1 copy.148
  236.8 0.1 dynamic-slice_bitcast_fusion
  236.9 0.1 broadcast_multiply_fusion.2
  237.0 0.1 broadcast_multiply_fusion.3
  237.1 0.7 broadcast_add_fusion
  237.8 19.2 %all-to-all-done.1 = f32[8,1,49152]{2,1,0:T(1,128)S(1)} async-done(((f32[8,1,49152]{2,1,0:T(1,128)}), f32[8,1,49152]{2,1,0:T(1,128)S(1)}, u32[]{:S(2)}, u32[]{:S(2)}) %all-to-all-start.1) | async-done | bytes 1572896 | tf_op jit(solution)/shard_map/all_to_all | solution.py:79
  257.0 0.5 broadcast.300
  257.5 4.4 reduce
  261.9 38.7 %reshape.389 = f32[4096,3,4,8]{3,2,1,0:T(4,128)} reshape(f32[8,49152]{1,0:T(8,128)S(1)} %reduce) | data formatting | bytes 3145728
  300.5 20.7 %copy.167 = f32[8,4,3,8,512]{4,0,3,2,1:T(8,128)} copy(f32[8,4,3,8,512]{0,1,2,4,3:T(4,128)} %bitcast.147) | data formatting | bytes 3145728 | tf_op jit(solution)/shard_map/all_to_all | solution.py:79
  321.2 2.6 reshape.305
  323.9 5.1 fusion.5
  329.0 3.2 fusion.2
  332.2 2.1 copy.149
  334.3 4.6 all-to-all-start.2
  338.9 0.6 broadcast_clamp_fusion
  339.6 19.9 %all-to-all-done.2 = f32[64,4,3,512]{3,1,2,0:T(4,128)S(1)} async-done(((f32[64,4,3,512]{3,1,2,0:T(4,128)}), f32[64,4,3,512]{3,1,2,0:T(4,128)S(1)}, u32[]{:S(2)}, u32[]{:S(2)}) %all-to-all-start.2) | async-done | bytes 1572896 | tf_op jit(solution)/shard_map/all_to_all | solution.py:92
  359.5 0.5 copy.182
  360.0 2.1 copy.170
  362.1 2.6 reshape.383
  364.7 5.1 fusion.35
  369.9 5.1 fusion.19
  375.0 2.7 fusion.58
  377.8 2.5 copy.154
  380.4 1.5 copy.155
  382.0 0.2 pad_maximum_fusion
  382.2 0.1 reshape_reshape.7
  382.4 160.3 %gather_fusion = f32[16384]{0:T(1024)} fusion(f32[24576]{0:T(1024)S(1)} %reshape_reshape.7, s32[16384]{0:T(1024)S(1)} %copy-done.8), kind=kCustom, calls=%fused_computation | custom fusion | bytes 196608 | tf_op jit(solution)/shard_map/gather | solution.py:96
  542.7 1.5 gather_fusion.1
  544.3 0.8 fusion.40
  545.1 96.7 %all-gather.3.cloned.1.call-done = f32[262144]{0:T(1024)} async-done(((f32[1024]{0:T(1024)}), f32[262144]{0:T(1024)}) %all-gather.3.cloned.1.call-update) | async-done | bytes 1048592 | tf_op jit(solution)/shard_map/all_gather | solution.py:143
  641.8 1.4 reshape.373
  643.2 0.1 reduce_sum.37
  643.3 5.6 convolution_bitcast_fusion
  649.0 0.2 convolution_bitcast_fusion.1
  649.2 2.2 scatter_fusion.1
  651.4 7.4 all-to-all-start.3
  658.9 0.6 fusion.51
  659.5 8.2 all-to-all-done.3
  667.7 45.5 %gather_fusion.3 = f32[8192]{0:T(1024)S(1)} fusion(f32[16384]{0:T(1024)S(1)} %bitcast.144, s32[8192]{0:T(1024)S(1)} %broadcast_clamp_fusion.1), kind=kCustom, calls=%fused_computation.3 | custom fusion | bytes 98304 | tf_op jit(solution)/shard_map/gather | solution.py:149
  713.2 45.5 %gather_fusion.2 = f32[8192]{0:T(1024)S(1)} fusion(f32[16384]{0:T(1024)S(1)} %bitcast.145, s32[8192]{0:T(1024)S(1)} %broadcast_clamp_fusion.2), kind=kCustom, calls=%fused_computation.2 | custom fusion | bytes 98304 | tf_op jit(solution)/shard_map/gather | solution.py:149
  758.8 0.6 multiply_reduce_fusion
  759.4 74.7 %all-reduce = (f32[]{:T(128)}, f32[]{:T(128)}) all-reduce(f32[]{:T(128)} %fusion.51, f32[]{:T(128)} %get-tuple-element.9), channel_id=1, replica_groups=mesh['group'=32,'pencil'=8] {'group','pencil'}, use_global_device_ids=true, to_apply=%region_1.0 | all-reduce | flops 2 | bytes 16 | tf_op jit(solution)/shard_map/psum | solution.py:127
  835.5 0.6 fusion.52
  836.1 73.4 %psum.23 = f32[]{:T(128)} all-reduce(f32[]{:T(128)} %get-tuple-element.7), channel_id=1, replica_groups=mesh['group'=32,'pencil'=8] {'group','pencil'}, use_global_device_ids=true, to_apply=%region_10.11 | all-reduce | flops 1 | bytes 8 | tf_op jit(solution)/shard_map/psum | solution.py:155
  910.8 0.7 multiply_add_fusion
  (55 shorter events, 0.5 us)
Async XLA Ops:
  8.2 64.0 %copy-start.1 = (s32[8192,1]{0,1:T(1,128)}, s32[8192,1]{0,1:T(1,128)S(1)}, u32[]{:S(2)}) copy-start(s32[8192,1]{0,1:T(1,128)S(1)} %get-tuple-element.19) | copy-start | bytes 98308
  8.2 64.0 %copy-start.9 = (s32[8192,1]{0,1:T(1,128)}, s32[8192,1]{0,1:T(1,128)S(1)}, u32[]{:S(2)}) copy-start(s32[8192,1]{0,1:T(1,128)S(1)} %get-tuple-element.20) | copy-start | bytes 98308
  40.2 44.0 %copy-start.11 = (s32[1,1,16384]{2,1,0:T(1,128)S(1)}, s32[1,1,16384]{2,1,0:T(1,128)}, u32[]{:S(2)}) copy-start(s32[1,1,16384]{2,1,0:T(1,128)} %param.20) | copy-start | bytes 196612
  40.2 114.0 %copy-start = (f32[4,3,64,64]{3,2,1,0:T(8,128)S(1)}, f32[4,3,64,64]{3,2,1,0:T(8,128)}, u32[]{:S(2)}) copy-start(f32[4,3,64,64]{3,2,1,0:T(8,128)} %param.16) | copy-start | bytes 589828
  72.1 20.9 %all-to-all-start = ((f32[32,1,512]{2,1,0:T(1,128)}), f32[32,1,512]{2,1,0:T(1,128)S(1)}, u32[]{:S(2)}, u32[]{:S(2)}) async-start(f32[32,1,512]{2,1,0:T(1,128)} %bitcast.11), calls=%async_computation | async-start | bytes 131072 | tf_op jit(solution)/shard_map/all_to_all | solution.py:135
  85.0 8.1 copy-start.6
  229.8 6.5 copy-start.12
  229.8 7.0 copy-start.15
  229.8 27.1 %all-to-all-start.1 = ((f32[8,1,49152]{2,1,0:T(1,128)}), f32[8,1,49152]{2,1,0:T(1,128)S(1)}, u32[]{:S(2)}, u32[]{:S(2)}) async-start(f32[8,1,49152]{2,1,0:T(1,128)} %reshape.388), calls=%async_computation.1 | async-start | bytes 3145728 | tf_op jit(solution)/shard_map/all_to_all | solution.py:79
  323.9 5.1 copy-start.13
  332.2 6.7 copy-start.16
  334.3 4.6 copy-start.7
  334.3 25.2 %all-to-all-start.2 = ((f32[64,4,3,512]{3,1,2,0:T(4,128)}), f32[64,4,3,512]{3,1,2,0:T(4,128)S(1)}, u32[]{:S(2)}, u32[]{:S(2)}) async-start(f32[64,4,3,512]{3,1,2,0:T(4,128)} %copy.149), calls=%async_computation.2 | async-start | bytes 3145728 | tf_op jit(solution)/shard_map/all_to_all | solution.py:92
  338.9 302.9 %all-gather.3.cloned.1.call-start = ((), (), s32[]{:S(2)}) async-start(), calls=%async_computation.4 | async-start | bytes 1052672 | tf_op jit(solution)/shard_map/all_gather | solution.py:143
  377.8 4.6 copy-start.8
  382.4 161.9 %copy-start.17 = (s32[1,1,32]{2,1,0:T(1,128)S(1)}, s32[1,1,32]{2,1,0:T(1,128)}, u32[]{:S(2)}) copy-start(s32[1,1,32]{2,1,0:T(1,128)} %param.23) | copy-start | bytes 388
  382.4 162.7 %copy-start.2 = (s32[8192,1]{0,1:T(1,128)S(1)}, s32[8192,1]{0,1:T(1,128)}, u32[]{:S(2)}) copy-start(s32[8192,1]{0,1:T(1,128)} %copy-done.1) | copy-start | bytes 98308
  643.2 15.6 %copy-start.10 = (s32[8192,1]{0,1:T(1,128)S(1)}, s32[8192,1]{0,1:T(1,128)}, u32[]{:S(2)}) copy-start(s32[8192,1]{0,1:T(1,128)} %copy-done.9) | copy-start | bytes 98308
  643.2 15.6 %copy-start.4 = (f32[1,1,8192]{2,1,0:T(1,128)S(1)}, f32[1,1,8192]{2,1,0:T(1,128)}, u32[]{:S(2)}) copy-start(f32[1,1,8192]{2,1,0:T(1,128)} %param.15) | copy-start | bytes 98308
  643.2 15.6 %copy-start.5 = (f32[1,1,8192]{2,1,0:T(1,128)S(1)}, f32[1,1,8192]{2,1,0:T(1,128)}, u32[]{:S(2)}) copy-start(f32[1,1,8192]{2,1,0:T(1,128)} %param.13) | copy-start | bytes 98308
  651.4 16.3 %all-to-all-start.3 = ((f32[32,1,512]{2,1,0:T(1,128)}), f32[32,1,512]{2,1,0:T(1,128)S(1)}, u32[]{:S(2)}, u32[]{:S(2)}) async-start(f32[32,1,512]{2,1,0:T(1,128)} %bitcast.57), calls=%async_computation.3 | async-start | bytes 131072 | tf_op jit(solution)/shard_map/all_to_all | solution.py:146
  713.2 45.6 %copy-start.3 = (f32[1,1,8192]{2,1,0:T(1,128)S(1)}, f32[1,1,8192]{2,1,0:T(1,128)}, u32[]{:S(2)}) copy-start(f32[1,1,8192]{2,1,0:T(1,128)} %param.14) | copy-start | bytes 98308
  713.2 197.6 %copy-start.14 = (f32[1,1,8192]{2,1,0:T(1,128)S(1)}, f32[1,1,8192]{2,1,0:T(1,128)}, u32[]{:S(2)}) copy-start(f32[1,1,8192]{2,1,0:T(1,128)} %param.12) | copy-start | bytes 98308
Sparse Core Ops, SparseCore 0:
  545.2 96.5 all-gather.2
